TPU v7x, 32 devices: a whole 2x2x4 slice. The times are simulated.
32 devices in a mesh: lat: 4 (over z), gx: 2 (over y), gy: 4 (over x, core).
Axes of the slice: x: 2, y: 2, z: 4, core: 2. Of those that a mesh axis runs over, the one named last changes fastest.
Arguments:
- latents: bfloat16 [256, 1024], P(('lat', 'gx', 'gy')), may hold values from -16 to 16
- w_key: bfloat16 [1024, 128], replicated, may hold values from -0.375 to 0.375
- w_value: bfloat16 [1024, 128], replicated, may hold values from -0.1875 to 0.1875
- queries: bfloat16 [64, 64, 8, 128], P(('lat', 'gx'), 'gy'), may hold values from -15 to 15
- conv_one: bfloat16 [3, 3, 64, 384], replicated, may hold values from -0.109375 to 0.109375
- bias_one: float32 [64], replicated, may hold values from -2.5 to 2.5
- conv_two: bfloat16 [3, 3, 64, 192], replicated, may hold values from -0.15625 to 0.15625
- bias_two: float32 [64], replicated, may hold values from -2.5 to 2.5
Outputs:
- voxel_out: bfloat16 [64, 64, 512], P(('lat', 'gx'), 'gy')
All inputs are finite; a program needn't handle non-finite values.
Results may differ from a plain program's by a relative error of at most 0.0097.
Values may be sent and summed in bfloat16 or wider, within the bound.
A program may use at most 64 MiB of HBM per device.

v0:
```python
from functools import partial
import math

import jax
import jax.numpy as jnp
from jax import lax
from jax.sharding import PartitionSpec as P


def with_halo(cells, sides, width):
    for axis, dim in sides:
        count = lax.axis_size(axis)
        ends = count - 1
        head = lax.slice_in_dim(cells, 0, width, axis=dim)
        tail = lax.slice_in_dim(cells, cells.shape[dim] - width, cells.shape[dim], axis=dim)
        cells = jnp.concatenate(
            [
                lax.ppermute(tail, axis, [(i, (i + 1) % count) for i in range(ends)]),
                cells,
                lax.ppermute(head, axis, [((i + 1) % count, i) for i in range(ends)]),
            ],
            axis=dim,
        )
    return cells


def fold_latents(state_all, pieces, offset, queries_flat, block_rows):
    key_piece, value_piece = pieces
    value_wide = value_piece.astype(jnp.float32)
    score_scale = 1.0 / math.sqrt(queries_flat.shape[1])
    block_count = queries_flat.shape[0] // block_rows

    def one_block(block_index, running):
        running_max, denominator, weighted = running
        row_start = block_index * block_rows
        query_rows = lax.dynamic_slice_in_dim(queries_flat, row_start, block_rows, 0)
        scores = (
            lax.dot_general(
                query_rows, key_piece, (((1,), (1,)), ((), ())), preferred_element_type=jnp.float32
            )
            * score_scale
        )
        old_max = lax.dynamic_slice_in_dim(running_max, row_start, block_rows, 0)
        new_max = jnp.maximum(old_max, jnp.max(scores, axis=1))
        factor = jnp.exp(old_max - new_max)
        weights = jnp.exp(scores - new_max[:, None])
        old_denominator = lax.dynamic_slice_in_dim(denominator, row_start, block_rows, 0)
        new_denominator = old_denominator * factor + jnp.sum(weights, axis=1)
        old_weighted = lax.dynamic_slice_in_dim(weighted, row_start, block_rows, 0)
        new_weighted = old_weighted * factor[:, None] + jnp.dot(
            weights, value_wide, precision=lax.Precision.HIGHEST, preferred_element_type=jnp.float32
        )
        running_max = lax.dynamic_update_slice_in_dim(running_max, new_max, row_start, 0)
        denominator = lax.dynamic_update_slice_in_dim(denominator, new_denominator, row_start, 0)
        weighted = lax.dynamic_update_slice_in_dim(weighted, new_weighted, row_start, 0)
        return (running_max, denominator, weighted)

    return lax.fori_loop(0, block_count, one_block, state_all)


def convolve_tile(volume, kernel, out_rows, out_cols, slab_cells, channels):
    shaped = volume.reshape(out_rows + 2, out_cols + 2, slab_cells, channels)
    padded = jnp.pad(shaped, ((0, 0), (0, 0), (1, 1), (0, 0)))
    result = None
    for tap_x in range(3):
        for tap_y in range(3):
            window = padded[tap_x : tap_x + out_rows, tap_y : tap_y + out_cols]
            stacked = jnp.concatenate(
                [window[:, :, tap_z : tap_z + slab_cells] for tap_z in range(3)], axis=-1
            )
            term = lax.dot_general(
                stacked.reshape(-1, 3 * channels),
                kernel[tap_x, tap_y],
                (((1,), (1,)), ((), ())),
                preferred_element_type=jnp.float32,
            )
            result = term if result is None else result + term
    return result


def shards(latents, w_key, w_value, queries, conv_one, bias_one, conv_two, bias_two):
    tile_rows, tile_cols, slab_cells, channels = queries.shape
    out_channels = conv_one.shape[2]
    key_rows = jnp.dot(latents, w_key, preferred_element_type=jnp.float32).astype(jnp.bfloat16)
    value_rows = jnp.dot(latents, w_value, preferred_element_type=jnp.float32).astype(jnp.bfloat16)
    queries_flat = queries.reshape(tile_rows * tile_cols * slab_cells, channels)
    voxel_count = queries_flat.shape[0]
    start_state = (
        jnp.full((voxel_count,), -jnp.inf, jnp.float32),
        jnp.zeros((voxel_count,), jnp.float32),
        jnp.zeros((voxel_count, channels), jnp.float32),
    )
    folder = partial(fold_latents, queries_flat=queries_flat, block_rows=math.gcd(voxel_count, 512))
    every_keys, every_values = (
        lax.all_gather(key_rows, ("lat", "gx", "gy"), axis=0, tiled=True),
        lax.all_gather(value_rows, ("lat", "gx", "gy"), axis=0, tiled=True),
    )
    running_max, denominator, weighted = folder(start_state, (every_keys, every_values), 0)
    attended = (
        (weighted / denominator[:, None])
        .astype(jnp.bfloat16)
        .reshape(tile_rows, tile_cols, slab_cells * channels)
    )
    padded_attended = with_halo(attended, ((("lat", "gx"), 0), ("gy", 1)), 1)
    pre_act = (
        convolve_tile(padded_attended, conv_one, tile_rows, tile_cols, slab_cells, channels)
        + bias_one
    )
    hidden = (
        jax.nn.silu(pre_act)
        .astype(jnp.bfloat16)
        .reshape(tile_rows, tile_cols, slab_cells * out_channels)
    )
    bordered = with_halo(hidden, ((("lat", "gx"), 0), ("gy", 1)), 1)
    final = (
        convolve_tile(bordered, conv_two, tile_rows, tile_cols, slab_cells, out_channels) + bias_two
    )
    return final.reshape(tile_rows, tile_cols, slab_cells * out_channels).astype(jnp.bfloat16)


def solution(mesh):
    return jax.shard_map(
        shards,
        mesh=mesh,
        in_specs=(
            P(("lat", "gx", "gy"), None),
            P(),
            P(),
            P(("lat", "gx"), "gy", None, None),
            P(),
            P(),
            P(),
            P(),
        ),
        out_specs=P(("lat", "gx"), "gy", None),
        check_vma=False,
    )
```

profile of v0, /device:TPU:0, one launch (start us, length us, event | category | flops | bytes accessed | tf_op | source)
XLA Modules:
  0.0 132.4 jit_solution(2027326712255306043)
XLA Ops:
  0.0 0.9 copy-done
  1.0 0.9 convolution_convert_fusion.1
  1.8 1.1 convolution_convert_fusion
  2.9 43.4 %all_gather.7 = bf16[256,128]{1,0:T(8,128)(2,1)S(1)} all-gather(bf16[8,128]{1,0:T(8,128)(2,1)S(1)} %convolution_convert_fusion), channel_id=1, replica_groups=mesh['lat'=4,'gx'=2,'gy'=4] {'lat','gx','gy'}, dimensions={0}, use_global_device_ids=true | all-gather | bytes 67584 | tf_op jit(solution)/shard_map/all_gather | solution.py:96
  46.3 36.8 %all_gather.6 = bf16[256,128]{1,0:T(8,128)(2,1)S(1)} all-gather(bf16[8,128]{1,0:T(8,128)(2,1)S(1)} %convolution_convert_fusion.1), channel_id=1, replica_groups=mesh['lat'=4,'gx'=2,'gy'=4] {'lat','gx','gy'}, dimensions={0}, use_global_device_ids=true | all-gather | bytes 67584 | tf_op jit(solution)/shard_map/all_gather | solution.py:95
  83.2 3.6 %while.17 = (s32[]{:T(128)}, f32[1024]{0:T(1024)S(1)}, f32[1024]{0:T(1024)S(1)}, f32[1024,128]{1,0:T(8,128)S(1)}, bf16[1024,128]{1,0:T(8,128)(2,1)S(1)}, /*index...) while((s32[]{:T(128)}, f32[1024]{0:T(1024)S(1)}, ...), condition=%wide.region_3.0_spmd, body=%wide.region_0.0_spmd.sunk | while | flops 235668480 | bytes 2472107 | solution.py:58
  84.0 1.0 fusion.89
  85.8 1.0 fusion.89
  87.0 1.3 collective-permute-start
  88.4 1.3 collective-permute-start.1
  89.9 4.2 %collective-permute-done.1 = bf16[1,16,1024]{2,1,0:T(8,128)(2,1)S(1)} collective-permute-done((bf16[1,16,1024]{2,1,0:T(8,128)(2,1)S(1)}, bf16[1,16,1024]{2,1,0:T(8,128)(2,1)S(1)}, u32[]{:S(2)}, u32[]{:S(2)}) %collective-permute-start.1) | collective-permute-done | bytes 32800 | tf_op jit(solution)/shard_map/ppermute | solution.py:20
  94.2 1.3 collective-permute-start.2
  95.5 1.3 collective-permute-start.3
  96.9 3.7 %collective-permute-done.3 = bf16[10,1,1024]{2,1,0:T(2,128)(2,1)S(1)} collective-permute-done((bf16[10,1,1024]{2,1,0:T(2,128)(2,1)S(1)}, bf16[10,1,1024]{2,1,0:T(2,128)(2,1)S(1)}, u32[]{:S(2)}, u32[]{:S(2)}) %collective-permute-start.3) | collective-permute-done | bytes 20512 | tf_op jit(solution)/shard_map/ppermute | solution.py:20
  101.3 1.2 pad_slice_fusion.19
  102.8 0.8 copy-done.2
  108.5 1.6 %collective-permute-start.4 = (bf16[1,16,512]{2,1,0:T(8,128)(2,1)S(1)}, bf16[1,16,512]{2,1,0:T(8,128)(2,1)S(1)}, u32[]{:S(2)}, u32[]{:S(2)}) collective-permute-start(bf16[1,16,512]{2,1,0:T(8,128)(2,1)S(1)} %slice.385), channel_id=1, source_target_pairs={{0,4},{4,8},{8,12},{12,16},{16,20},{20,24},{24,28},{1,5},{5,9},{9,... | collective-permute-start | bytes 49160 | tf_op jit(solution)/shard_map/ppermute | solution.py:18
  110.6 1.3 collective-permute-start.5
  112.1 4.1 %collective-permute-done.5 = bf16[1,16,512]{2,1,0:T(8,128)(2,1)S(1)} collective-permute-done((bf16[1,16,512]{2,1,0:T(8,128)(2,1)S(1)}, bf16[1,16,512]{2,1,0:T(8,128)(2,1)S(1)}, u32[]{:S(2)}, u32[]{:S(2)}) %collective-permute-start.5) | collective-permute-done | bytes 16416 | tf_op jit(solution)/shard_map/ppermute | solution.py:20
  116.2 3.2 %collective-permute-start.6 = (bf16[10,1,512]{2,1,0:T(2,128)(2,1)S(1)}, bf16[10,1,512]{2,1,0:T(2,128)(2,1)S(1)}, u32[]{:S(2)}, u32[]{:S(2)}) collective-permute-start(bf16[10,1,512]{2,1,0:T(2,128)(2,1)S(1)} %get-tuple-element.210), channel_id=1, source_target_pairs={{0,1},{1,2},{2,3},{4,5},{5,6},{6,7},{8,9},{9,10},{10,11},{12,13},{... | collective-permute-start | bytes 30728 | tf_op jit(solution)/shard_map/ppermute | solution.py:18
  119.4 1.5 %collective-permute-start.7 = (bf16[10,1,512]{2,1,0:T(2,128)(2,1)S(1)}, bf16[10,1,512]{2,1,0:T(2,128)(2,1)S(1)}, u32[]{:S(2)}, u32[]{:S(2)}) collective-permute-start(bf16[10,1,512]{2,1,0:T(2,128)(2,1)S(1)} %get-tuple-element.211), channel_id=1, source_target_pairs={{1,0},{2,1},{3,2},{5,4},{6,5},{7,6},{9,8},{10,9},{11,10},{13,12},{... | collective-permute-start | bytes 30728 | tf_op jit(solution)/shard_map/ppermute | solution.py:20
  120.9 2.5 %collective-permute-done.7 = bf16[10,1,512]{2,1,0:T(2,128)(2,1)S(1)} collective-permute-done((bf16[10,1,512]{2,1,0:T(2,128)(2,1)S(1)}, bf16[10,1,512]{2,1,0:T(2,128)(2,1)S(1)}, u32[]{:S(2)}, u32[]{:S(2)}) %collective-permute-start.7) | collective-permute-done | bytes 10272 | tf_op jit(solution)/shard_map/ppermute | solution.py:20
  124.1 1.2 pad_slice_fusion.1
  131.5 0.9 convert_element_type.31
  (89 shorter events, 15.4 us)
Async XLA Ops:
  0.0 1.0 copy-start
  0.0 83.2 %copy-start.1 = (bf16[8,16,8,128]{3,2,1,0:T(8,128)(2,1)S(1)}, bf16[8,16,8,128]{3,2,1,0:T(8,128)(2,1)}, u32[]{:S(2)}) copy-start(bf16[8,16,8,128]{3,2,1,0:T(8,128)(2,1)} %param.13) | copy-start | bytes 786436
  87.0 2.9 %collective-permute-start = (bf16[1,16,1024]{2,1,0:T(8,128)(2,1)S(1)}, bf16[1,16,1024]{2,1,0:T(8,128)(2,1)S(1)}, u32[]{:S(2)}, u32[]{:S(2)}) collective-permute-start(bf16[1,16,1024]{2,1,0:T(8,128)(2,1)S(1)} %slice.343), channel_id=1, source_target_pairs={{0,4},{4,8},{8,12},{12,16},{16,20},{20,24},{24,28},{1,5},{5,9},{9,... | collective-permute-start | bytes 98312 | tf_op jit(solution)/shard_map/ppermute | solution.py:18
  88.4 5.8 %collective-permute-start.1 = (bf16[1,16,1024]{2,1,0:T(8,128)(2,1)S(1)}, bf16[1,16,1024]{2,1,0:T(8,128)(2,1)S(1)}, u32[]{:S(2)}, u32[]{:S(2)}) collective-permute-start(bf16[1,16,1024]{2,1,0:T(8,128)(2,1)S(1)} %slice.345), channel_id=1, source_target_pairs={{4,0},{8,4},{12,8},{16,12},{20,16},{24,20},{28,24},{5,1},{9,5},{13... | collective-permute-start | bytes 98312 | tf_op jit(solution)/shard_map/ppermute | solution.py:20
  94.2 2.6 %collective-permute-start.2 = (bf16[10,1,1024]{2,1,0:T(2,128)(2,1)S(1)}, bf16[10,1,1024]{2,1,0:T(2,128)(2,1)S(1)}, u32[]{:S(2)}, u32[]{:S(2)}) collective-permute-start(bf16[10,1,1024]{2,1,0:T(2,128)(2,1)S(1)} %get-tuple-element.206), channel_id=1, source_target_pairs={{0,1},{1,2},{2,3},{4,5},{5,6},{6,7},{8,9},{9,10},{10,11},{12,13},{... | collective-permute-start | bytes 61448 | tf_op jit(solution)/shard_map/ppermute | solution.py:18
  95.5 5.0 %collective-permute-start.3 = (bf16[10,1,1024]{2,1,0:T(2,128)(2,1)S(1)}, bf16[10,1,1024]{2,1,0:T(2,128)(2,1)S(1)}, u32[]{:S(2)}, u32[]{:S(2)}) collective-permute-start(bf16[10,1,1024]{2,1,0:T(2,128)(2,1)S(1)} %get-tuple-element.207), channel_id=1, source_target_pairs={{1,0},{2,1},{3,2},{5,4},{6,5},{7,6},{9,8},{10,9},{11,10},{13,12},{... | collective-permute-start | bytes 61448 | tf_op jit(solution)/shard_map/ppermute | solution.py:20
  102.5 1.0 copy-start.2
  107.2 0.7 copy-start.5
  108.5 3.5 %collective-permute-start.4 = (bf16[1,16,512]{2,1,0:T(8,128)(2,1)S(1)}, bf16[1,16,512]{2,1,0:T(8,128)(2,1)S(1)}, u32[]{:S(2)}, u32[]{:S(2)}) collective-permute-start(bf16[1,16,512]{2,1,0:T(8,128)(2,1)S(1)} %slice.385), channel_id=1, source_target_pairs={{0,4},{4,8},{8,12},{12,16},{16,20},{20,24},{24,28},{1,5},{5,9},{9,... | collective-permute-start | bytes 49160 | tf_op jit(solution)/shard_map/ppermute | solution.py:18
  110.6 5.6 %collective-permute-start.5 = (bf16[1,16,512]{2,1,0:T(8,128)(2,1)S(1)}, bf16[1,16,512]{2,1,0:T(8,128)(2,1)S(1)}, u32[]{:S(2)}, u32[]{:S(2)}) collective-permute-start(bf16[1,16,512]{2,1,0:T(8,128)(2,1)S(1)} %slice.387), channel_id=1, source_target_pairs={{4,0},{8,4},{12,8},{16,12},{20,16},{24,20},{28,24},{5,1},{9,5},{13... | collective-permute-start | bytes 49160 | tf_op jit(solution)/shard_map/ppermute | solution.py:20
  116.2 4.7 %collective-permute-start.6 = (bf16[10,1,512]{2,1,0:T(2,128)(2,1)S(1)}, bf16[10,1,512]{2,1,0:T(2,128)(2,1)S(1)}, u32[]{:S(2)}, u32[]{:S(2)}) collective-permute-start(bf16[10,1,512]{2,1,0:T(2,128)(2,1)S(1)} %get-tuple-element.210), channel_id=1, source_target_pairs={{0,1},{1,2},{2,3},{4,5},{5,6},{6,7},{8,9},{9,10},{10,11},{12,13},{... | collective-permute-start | bytes 30728 | tf_op jit(solution)/shard_map/ppermute | solution.py:18
  119.4 4.0 %collective-permute-start.7 = (bf16[10,1,512]{2,1,0:T(2,128)(2,1)S(1)}, bf16[10,1,512]{2,1,0:T(2,128)(2,1)S(1)}, u32[]{:S(2)}, u32[]{:S(2)}) collective-permute-start(bf16[10,1,512]{2,1,0:T(2,128)(2,1)S(1)} %get-tuple-element.211), channel_id=1, source_target_pairs={{1,0},{2,1},{3,2},{5,4},{6,5},{7,6},{9,8},{10,9},{11,10},{13,12},{... | collective-permute-start | bytes 30728 | tf_op jit(solution)/shard_map/ppermute | solution.py:20
  125.3 1.0 copy-start.3
  130.4 0.7 copy-start.4
where the time goes:
time: 135 us; the launch traced here: 132 us
  blocking collectives  80.2 us (59%)
  waiting for transfers between devices  14.7 us (11%)
  starting transfers between devices  12.7 us (9%)
  matrix products  10.3 us (8%)
  local copies, waits for them, and re-layouts  9.04 us (7%)
  other arithmetic  4.9 us (4%)
    all_gather x1, blocking collectives, shards(): lax.all_gather(value_rows, ('lat', 'gx', 'gy'), axis=0, tiled=True)  43.4 us
    all_gather x1, blocking collectives, shards(): lax.all_gather(key_rows, ('lat', 'gx', 'gy'), axis=0, tiled=True)  36.8 us
    ppermute x4, waiting for transfers between devices, with_halo(): lax.ppermute(head, axis, [((i + 1) % count, i) for i in range(ends)])  14.6 us
    ppermute x4, starting transfers between devices, with_halo(): lax.ppermute(tail, axis, [(i, (i + 1) % count) for i in range(ends)])  7.38 us
    dot_general x18, matrix products, convolve_tile(): lax.dot_general(stacked.reshape(-1, 3 * channels), kernel[tap_x, tap_y],...  5.82 us
    ppermute x4, starting transfers between devices, with_halo(): lax.ppermute(head, axis, [((i + 1) % count, i) for i in range(ends)])  5.35 us
    concatenate x14, other arithmetic, convolve_tile(): jnp.concatenate([window[:, :, tap_z:tap_z + slab_cells] for tap_z in rang...  3.42 us
    unnamed x16, local copies, waits for them, and re-layouts  3.37 us
  transfers between devices with their start and end apart: 8, of which 5 were waited for; matrix products, arithmetic and copies ran while one was open for 1% of the time, Pallas kernels for 0%

commit v1 on v0

v1 whole, which is shorter than its diff:
```python
from functools import partial
import math

import jax
import jax.numpy as jnp
from jax import lax
from jax.experimental import pallas as pl
from jax.experimental.pallas import tpu as pltpu
from jax.sharding import PartitionSpec as P

MESH = pl.DeviceIdType.MESH
DIRECTIONS = [(dx, dy) for dx in (-1, 0, 1) for dy in (-1, 0, 1) if (dx, dy) != (0, 0)]
BF16 = jnp.bfloat16
F32 = jnp.float32
NT = (((1,), (1,)), ((), ()))


def kernel(
    sizes, latents, w_key, w_value, queries, conv_one, bias_one, conv_two, bias_two, out,
    latents_v, wk_v, wv_v, q_pad, c1_v, b1_v, c2_v, b2_v, kv, att3, hid3, result,
    local_sem, halo_send, halo_recv, col_send, col_recv, plane_send, plane_recv, keys, values,
):
    n_lat, n_gx, n_gy, rows, cols, slab = sizes
    lat, gx, gy = lax.axis_index("lat"), lax.axis_index("gx"), lax.axis_index("gy")
    n_plane = n_gx * n_gy
    plane = gx * n_gy + gy
    n_row_tiles = n_lat * n_gx
    row_tile = lat * n_gx + gx
    wide = cols * slab
    edge = 2 * slab

    def device_of(tile_x, tile_y):
        return (tile_x // n_gx, tile_x % n_gx, tile_y)

    def present(tile_x, tile_y):
        return (tile_x >= 0) & (tile_x < n_row_tiles) & (tile_y >= 0) & (tile_y < n_gy)

    def plane_device(index):
        return (lat, index // n_gy, index % n_gy)

    loads = [
        pltpu.make_async_copy(src, dst, local_sem.at[i])
        for i, (src, dst) in enumerate([
            (latents, latents_v),
            (w_key, wk_v),
            (w_value, wv_v),
            (queries, q_pad.at[pl.ds(2, rows), pl.ds(edge, wide)]),
            (conv_one, c1_v),
            (bias_one, b1_v),
            (conv_two, c2_v),
            (bias_two, b2_v),
        ])
    ]
    for load in loads:
        load.start()

    barrier = pltpu.get_barrier_semaphore()
    awaited = n_lat - 1 + n_plane - 1
    for k in range(1, n_lat):
        pl.semaphore_signal(barrier, inc=1, device_id=((lat + k) % n_lat, gx, gy), device_id_type=MESH)
    for k in range(1, n_plane):
        pl.semaphore_signal(barrier, inc=1, device_id=plane_device((plane + k) % n_plane), device_id_type=MESH)
    for dx, dy in DIRECTIONS:
        there = present(row_tile + dx, gy + dy)
        awaited = awaited + there.astype(jnp.int32)

        @pl.when(there)
        def _():
            pl.semaphore_signal(
                barrier, inc=1, device_id=device_of(row_tile + dx, gy + dy), device_id_type=MESH
            )

    for load in loads[:3]:
        load.wait()
    lat_rows = latents_v[...]
    key_rows = jnp.dot(lat_rows, wk_v[...], preferred_element_type=F32).astype(BF16)
    value_rows = jnp.dot(lat_rows, wv_v[...], preferred_element_type=F32).astype(BF16)
    kv[plane, lat] = jnp.concatenate([key_rows, value_rows], axis=1)

    pl.semaphore_wait(barrier, awaited)

    def column_copy(k, owner):
        slot = kv.at[plane, owner]
        return pltpu.make_async_remote_copy(
            src_ref=slot, dst_ref=slot, send_sem=col_send.at[k], recv_sem=col_recv.at[k],
            device_id=((lat + k) % n_lat, gx, gy), device_id_type=MESH,
        )

    def plane_copy(k, owner):
        slot = kv.at[owner]
        return pltpu.make_async_remote_copy(
            src_ref=slot, dst_ref=slot, send_sem=plane_send.at[k], recv_sem=plane_recv.at[k],
            device_id=plane_device((plane + k) % n_plane), device_id_type=MESH,
        )

    def halo_copy(i, dx, dy):
        src_x = {1: rows - 2, -1: 0, 0: 0}[dx]
        dst_x = {1: 0, -1: rows + 2, 0: 2}[dx]
        src_y = {1: wide - edge, -1: 0, 0: 0}[dy]
        dst_y = {1: 0, -1: wide + edge, 0: edge}[dy]
        size_x, size_y = (rows if dx == 0 else 2), (wide if dy == 0 else edge)
        return pltpu.make_async_remote_copy(
            src_ref=queries.at[pl.ds(src_x, size_x), pl.ds(src_y, size_y)],
            dst_ref=q_pad.at[pl.ds(dst_x, size_x), pl.ds(dst_y, size_y)],
            send_sem=halo_send.at[i], recv_sem=halo_recv.at[i],
            device_id=device_of(row_tile + dx, gy + dy), device_id_type=MESH,
        )

    for k in range(1, n_lat):
        column_copy(k, lat).start()
    for i, (dx, dy) in enumerate(DIRECTIONS):
        @pl.when(present(row_tile + dx, gy + dy))
        def _():
            halo_copy(i, dx, dy).start()

    for k in range(1, n_lat):
        column_copy(k, (lat + n_lat - k) % n_lat).wait_recv()
    for k in range(1, n_plane):
        plane_copy(k, plane).start()

    for load in loads[3:]:
        load.wait()
    for i, (dx, dy) in enumerate(DIRECTIONS):
        @pl.when(present(row_tile - dx, gy - dy))
        def _():
            halo_copy(i, dx, dy).wait_recv()

    for k in range(1, n_plane):
        plane_copy(k, (plane + n_plane - k) % n_plane).wait_recv()

    n_all = n_plane * n_lat * kv.shape[2]
    channels = q_pad.shape[2]
    block = min(n_all, 256)
    piece_planes = block // (n_lat * kv.shape[2])
    for first in range(0, n_plane, piece_planes):
        every = kv[pl.ds(first, piece_planes)].reshape(block, 2 * channels)
        spot = pl.ds(first * n_lat * kv.shape[2], block)
        keys[spot, :] = every[:, :channels]
        values[spot, :channels] = every[:, channels:]
        values[spot, channels:] = jnp.ones((block, channels), BF16)
    exponent_scale = math.log2(math.e) / math.sqrt(channels)
    padded = wide + 2 * edge

    def shifted(cells):
        level = lax.broadcasted_iota(jnp.int32, cells.shape, 1)
        below = jnp.where(level == 0, 0.0, pltpu.roll(cells, 1, 1))
        above = jnp.where(level == slab - 1, 0.0, pltpu.roll(cells, slab - 1, 1))
        return below, above

    def attend(first, count):
        q = q_pad[pl.ds(first, count)].reshape(count * padded, channels)

        def fold(first_latent, state):
            spot = pl.ds(first_latent, block)
            scores = lax.dot_general(q, keys[spot, :], NT, preferred_element_type=F32)
            top = jnp.max(scores, axis=1, keepdims=True)
            if state is not None:
                top = jnp.maximum(top, state[0])
            weights = jnp.exp2((scores - top) * exponent_scale).astype(BF16)
            mixed = jnp.dot(weights, values[spot, :], preferred_element_type=F32)
            if state is not None:
                mixed = mixed + state[1] * jnp.exp2((state[0] - top) * exponent_scale)
            return top, mixed

        state = fold(0, None)
        if n_all > block:
            state = lax.fori_loop(
                1, n_all // block, lambda i, held: fold(pl.multiple_of(i * block, block), held), state
            )
        mixed = state[1]
        cells = (mixed[:, :channels] / mixed[:, channels:]).reshape(-1, slab, channels)
        below, above = shifted(cells)
        for c, part in enumerate((below, cells, above)):
            att3[pl.ds(first, count), :, c * channels : (c + 1) * channels] = (
                part.astype(BF16).reshape(count, padded, channels)
            )

    step = max(1, min(4, 1024 // n_all))
    steps = (rows + 4) // step
    if steps <= 4:
        for s in range(steps):
            attend(s * step, step)
    else:
        @pl.loop(0, steps)
        def _(s):
            attend(s * step, step)

    def blank(when, ref, index):
        @pl.when(when)
        def _():
            view = ref.at[index]
            view[...] = jnp.zeros(view.shape, ref.dtype)

    every_dim = slice(None)
    blank(row_tile == 0, att3, (pl.ds(0, 2), every_dim, every_dim))
    blank(row_tile == n_row_tiles - 1, att3, (pl.ds(rows + 2, 2), every_dim, every_dim))
    blank(gy == 0, att3, (every_dim, pl.ds(0, edge), every_dim))
    blank(gy == n_gy - 1, att3, (every_dim, pl.ds(wide + edge, edge), every_dim))

    def convolve(ref, weight, first, count, mid):
        length = ref.shape[1]
        total = None
        for a in range(3):
            cells = ref[pl.ds(first + a, count)].reshape(count * length, ref.shape[2])
            term = lax.dot_general(cells, weight[a], NT, preferred_element_type=F32)
            total = term if total is None else total + term
        total = total.reshape(count, length, 3 * mid)
        kept = length - 2 * slab
        return (
            total[:, :kept, :mid]
            + total[:, slab : slab + kept, mid : 2 * mid]
            + total[:, 2 * slab :, 2 * mid :]
        )

    mid = b1_v.shape[1]
    for first in range(0, rows + 2, 5):
        count = min(5, rows + 2 - first)
        half = (convolve(att3, c1_v, first, count, mid) + b1_v[...]) * 0.5
        cells = (half + half * jnp.tanh(half)).reshape(-1, slab, mid)
        below, above = shifted(cells)
        stacked = jnp.concatenate([below, cells, above], axis=2).astype(BF16)
        hid3[pl.ds(first, count)] = stacked.reshape(count, wide + edge, 3 * mid)

    blank(row_tile == 0, hid3, (pl.ds(0, 1), every_dim, every_dim))
    blank(row_tile == n_row_tiles - 1, hid3, (pl.ds(rows + 1, 1), every_dim, every_dim))
    blank(gy == 0, hid3, (every_dim, pl.ds(0, slab), every_dim))
    blank(gy == n_gy - 1, hid3, (every_dim, pl.ds(wide + slab, slab), every_dim))

    for first in range(0, rows, 4):
        final = convolve(hid3, c2_v, first, 4, mid) + b2_v[...]
        result[pl.ds(first * wide, 4 * wide), :mid] = final.reshape(4 * wide, mid)
    pieces = [result[pl.ds(z, rows * cols, stride=slab), :][:, :mid] for z in range(slab)]
    out[...] = jnp.concatenate(pieces, axis=1).astype(BF16)

    for k in range(1, n_lat):
        column_copy(k, lat).wait_send()
    for k in range(1, n_plane):
        plane_copy(k, plane).wait_send()
    for i, (dx, dy) in enumerate(DIRECTIONS):
        @pl.when(present(row_tile + dx, gy + dy))
        def _():
            halo_copy(i, dx, dy).wait_send()


def shards(sizes, latents, w_key, w_value, queries, conv_one, bias_one, conv_two, bias_two):
    rows, cols, slab, channels = queries.shape
    mid = conv_one.shape[2]
    n_lat, n_gx, n_gy = sizes
    piece = latents.shape[0]
    n_plane = n_gx * n_gy
    any_spec = pl.BlockSpec(memory_space=pl.ANY)
    operands = (
        latents, w_key, w_value,
        queries.reshape(rows, cols * slab, channels),
        conv_one.reshape(3, 3 * mid, 3 * channels),
        bias_one.reshape(1, mid),
        conv_two.reshape(3, 3 * mid, 3 * mid),
        bias_two.reshape(1, mid),
    )
    result = pl.pallas_call(
        partial(kernel, (n_lat, n_gx, n_gy, rows, cols, slab)),
        out_shape=jax.ShapeDtypeStruct((rows * cols, slab * mid), BF16),
        in_specs=[any_spec] * 8,
        out_specs=pl.BlockSpec(memory_space=pltpu.VMEM),
        scratch_shapes=[
            pltpu.VMEM(latents.shape, BF16),
            pltpu.VMEM(w_key.shape, BF16),
            pltpu.VMEM(w_value.shape, BF16),
            pltpu.VMEM((rows + 4, (cols + 4) * slab, channels), BF16),
            pltpu.VMEM(operands[4].shape, BF16),
            pltpu.VMEM((1, mid), F32),
            pltpu.VMEM(operands[6].shape, BF16),
            pltpu.VMEM((1, mid), F32),
            pltpu.VMEM((n_plane, n_lat, piece, 2 * channels), BF16),
            pltpu.VMEM((rows + 4, (cols + 4) * slab, 3 * channels), BF16),
            pltpu.VMEM((rows + 2, (cols + 2) * slab, 3 * mid), BF16),
            pltpu.VMEM((rows * cols * slab, 2 * mid), F32),
            pltpu.SemaphoreType.DMA((8,)),
            pltpu.SemaphoreType.DMA((8,)),
            pltpu.SemaphoreType.DMA((8,)),
            pltpu.SemaphoreType.DMA((n_lat,)),
            pltpu.SemaphoreType.DMA((n_lat,)),
            pltpu.SemaphoreType.DMA((n_plane,)),
            pltpu.SemaphoreType.DMA((n_plane,)),
            pltpu.VMEM((n_plane * n_lat * piece, channels), BF16),
            pltpu.VMEM((n_plane * n_lat * piece, 2 * channels), BF16),
        ],
        compiler_params=pltpu.CompilerParams(collective_id=0, has_side_effects=True),
    )(*operands)
    return result.reshape(rows, cols, slab * mid)


def solution(mesh):
    sizes = tuple(mesh.shape[name] for name in ("lat", "gx", "gy"))
    return jax.shard_map(
        partial(shards, sizes),
        mesh=mesh,
        in_specs=(
            P(("lat", "gx", "gy"), None),
            P(),
            P(),
            P(("lat", "gx"), "gy", None, None),
            P(),
            P(),
            P(),
            P(),
        ),
        out_specs=P(("lat", "gx"), "gy", None),
        check_vma=False,
    )
```

time: 135 us -> 18.5 us (0.14); the launches traced: 132 us -> 18.3 us
  blocking collectives: 80.2 us -> 0 us
  Pallas kernels: 0 us -> 16.7 us
  waiting for transfers between devices: 14.7 us -> 0 us
  starting transfers between devices: 12.7 us -> 0 us
  matrix products: 10.3 us -> 0 us
  local copies, waits for them, and re-layouts: 9.04 us -> 1.57 us
  other arithmetic: 4.9 us -> 0 us
    all_gather x2 -> x0, blocking collectives: 80.2 us -> none  [the longest x1 43.4 us: shards(): lax.all_gather(value_rows, ('lat', 'gx', 'gy'), axis=0, tiled=True)]
    pallas_call x0 -> x1, Pallas kernels: none -> 16.7 us  [shards(): pl.pallas_call(partial(kernel, (n_lat, n_gx, n_gy, rows, cols, slab)), ou...]
    ppermute x8 -> x0, waiting for transfers between devices: 14.7 us -> none  [the longest x4 14.6 us: with_halo(): lax.ppermute(head, axis, [((i + 1) % count, i) for i in range(ends)])]
    ppermute x8 -> x0, starting transfers between devices: 12.7 us -> none  [the longest x4 7.38 us: with_halo(): lax.ppermute(tail, axis, [(i, (i + 1) % count) for i in range(ends)])]
    dot_general x24 -> x0, matrix products: 10.3 us -> none  [the longest x18 5.82 us: convolve_tile(): lax.dot_general(stacked.reshape(-1, 3 * channels), kernel[tap_x, tap_y],...]
    concatenate x16 -> x0, other arithmetic: 3.73 us -> none  [the longest x14 3.42 us: convolve_tile(): jnp.concatenate([window[:, :, tap_z:tap_z + slab_cells] for tap_z in rang...]
    slice x14 -> x0, local copies, waits for them, and re-layouts: 3.65 us -> none  [the longest x4 3.04 us: convolve_tile(): window[:, :, tap_z:tap_z + slab_cells]]
    unnamed x16 -> x1, local copies, waits for them, and re-layouts: 3.37 us -> 1.57 us
  transfers between devices with their start and end apart: 8 -> 0, of which waited for: 5 -> 0; matrix products, arithmetic and copies ran while one was open for 1% -> 0% of each run, Pallas kernels for 0% -> 0%
where the time goes in v1:
time: 18.5 us; the launch traced here: 18.3 us
  Pallas kernels  16.7 us (90%)
  local copies, waits for them, and re-layouts  1.57 us (8%)
    pallas_call x1, Pallas kernels, shards(): pl.pallas_call(partial(kernel, (n_lat, n_gx, n_gy, rows, cols, slab)), ou...  16.7 us
    unnamed x1, local copies, waits for them, and re-layouts  1.57 us

profile of v1, /device:TPU:0, one launch (start us, length us, event | category | flops | bytes accessed | tf_op | source)
XLA Modules:
  0.0 18.3 jit_solution(17989498665909093547)
XLA Ops:
  0.0 16.7 %shard_map.82 = bf16[128,512]{1,0:T(8,128)(2,1)} custom-call(bf16[8,1024]{1,0:T(8,128)(2,1)} %latents.1, bf16[1024,128]{1,0:T(8,128)(2,1)} %w_key.1, bf16[1024,128]{1,0:T(8,128)(2,1)} %w_value.1, bf16[8,128,128]{2,1,0:T(8,128)(2,1)} %bitcast.9, bf16[3,192,384]{2,1,0:T(8,128)(2,1)} %bitcast.7, f32[1,64]{1,0:T(1,128)} %bitcast.10, ...), custom_call_target="tpu_custom_call" | custom-call | tf_op jit(solution)/shard_map/pallas_call | solution.py:260
  16.7 1.6 %copy.10 = bf16[8,16,512]{2,1,0:T(8,128)(2,1)} copy(bf16[8,16,512]{2,1,0:T(8,128)(2,1)} %bitcast.6) | data formatting | bytes 262144

commit v2 on v1

--- a/solution.py
+++ b/solution.py
@@ -18,7 +18,7 @@
 def kernel(
     sizes, latents, w_key, w_value, queries, conv_one, bias_one, conv_two, bias_two, out,
     latents_v, wk_v, wv_v, q_pad, c1_v, b1_v, c2_v, b2_v, kv, att3, hid3, result,
-    local_sem, halo_send, halo_recv, col_send, col_recv, plane_send, plane_recv, keys, values,
+    local_sem, halo_send, halo_recv, col_send, col_recv, plane_send, plane_recv, keys, values, c1_t, c2_t,
 ):
     n_lat, n_gx, n_gy, rows, cols, slab = sizes
     lat, gx, gy = lax.axis_index("lat"), lax.axis_index("gx"), lax.axis_index("gy")
@@ -30,13 +30,13 @@
     edge = 2 * slab
 
     def device_of(tile_x, tile_y):
-        return (tile_x // n_gx, tile_x % n_gx, tile_y)
+        return (lax.div(tile_x, n_gx), lax.rem(tile_x, n_gx), tile_y)
 
     def present(tile_x, tile_y):
         return (tile_x >= 0) & (tile_x < n_row_tiles) & (tile_y >= 0) & (tile_y < n_gy)
 
     def plane_device(index):
-        return (lat, index // n_gy, index % n_gy)
+        return (lat, lax.div(index, n_gy), lax.rem(index, n_gy))
 
     loads = [
         pltpu.make_async_copy(src, dst, local_sem.at[i])
@@ -51,15 +51,15 @@
             (bias_two, b2_v),
         ])
     ]
-    for load in loads:
+    for load in loads[:3]:
         load.start()
 
     barrier = pltpu.get_barrier_semaphore()
     awaited = n_lat - 1 + n_plane - 1
     for k in range(1, n_lat):
-        pl.semaphore_signal(barrier, inc=1, device_id=((lat + k) % n_lat, gx, gy), device_id_type=MESH)
+        pl.semaphore_signal(barrier, inc=1, device_id=(lax.rem(lat + k, n_lat), gx, gy), device_id_type=MESH)
     for k in range(1, n_plane):
-        pl.semaphore_signal(barrier, inc=1, device_id=plane_device((plane + k) % n_plane), device_id_type=MESH)
+        pl.semaphore_signal(barrier, inc=1, device_id=plane_device(lax.rem(plane + k, n_plane)), device_id_type=MESH)
     for dx, dy in DIRECTIONS:
         there = present(row_tile + dx, gy + dy)
         awaited = awaited + there.astype(jnp.int32)
@@ -70,6 +70,8 @@
                 barrier, inc=1, device_id=device_of(row_tile + dx, gy + dy), device_id_type=MESH
             )
 
+    for load in loads[3:]:
+        load.start()
     for load in loads[:3]:
         load.wait()
     lat_rows = latents_v[...]
@@ -83,14 +85,14 @@
         slot = kv.at[plane, owner]
         return pltpu.make_async_remote_copy(
             src_ref=slot, dst_ref=slot, send_sem=col_send.at[k], recv_sem=col_recv.at[k],
-            device_id=((lat + k) % n_lat, gx, gy), device_id_type=MESH,
+            device_id=(lax.rem(lat + k, n_lat), gx, gy), device_id_type=MESH,
         )
 
     def plane_copy(k, owner):
         slot = kv.at[owner]
         return pltpu.make_async_remote_copy(
             src_ref=slot, dst_ref=slot, send_sem=plane_send.at[k], recv_sem=plane_recv.at[k],
-            device_id=plane_device((plane + k) % n_plane), device_id_type=MESH,
+            device_id=plane_device(lax.rem(plane + k, n_plane)), device_id_type=MESH,
         )
 
     def halo_copy(i, dx, dy):
@@ -114,19 +116,23 @@
             halo_copy(i, dx, dy).start()
 
     for k in range(1, n_lat):
-        column_copy(k, (lat + n_lat - k) % n_lat).wait_recv()
+        column_copy(k, lax.rem(lat + n_lat - k, n_lat)).wait_recv()
     for k in range(1, n_plane):
         plane_copy(k, plane).start()
 
     for load in loads[3:]:
         load.wait()
+    for turned, weight in ((c1_t, c1_v), (c2_t, c2_v)):
+        depth = weight.shape[2]
+        for a in range(3):
+            turned[a * depth : (a + 1) * depth, :] = weight[a].T
     for i, (dx, dy) in enumerate(DIRECTIONS):
         @pl.when(present(row_tile - dx, gy - dy))
         def _():
             halo_copy(i, dx, dy).wait_recv()
 
     for k in range(1, n_plane):
-        plane_copy(k, (plane + n_plane - k) % n_plane).wait_recv()
+        plane_copy(k, lax.rem(plane + n_plane - k, n_plane)).wait_recv()
 
     n_all = n_plane * n_lat * kv.shape[2]
     channels = q_pad.shape[2]
@@ -198,11 +204,14 @@
     blank(gy == n_gy - 1, att3, (every_dim, pl.ds(wide + edge, edge), every_dim))
 
     def convolve(ref, weight, first, count, mid):
-        length = ref.shape[1]
+        length, depth = ref.shape[1:]
+        taps = [ref[pl.ds(first + a, count)].reshape(count * length, depth) for a in range(3)]
+        if depth % 128 == 0:
+            taps = [jnp.concatenate(taps, axis=1)]
         total = None
-        for a in range(3):
-            cells = ref[pl.ds(first + a, count)].reshape(count * length, ref.shape[2])
-            term = lax.dot_general(cells, weight[a], NT, preferred_element_type=F32)
+        for a, cells in enumerate(taps):
+            part = weight[a * depth : a * depth + cells.shape[1], :]
+            term = jnp.dot(cells, part, preferred_element_type=F32)
             total = term if total is None else total + term
         total = total.reshape(count, length, 3 * mid)
         kept = length - 2 * slab
@@ -215,7 +224,7 @@
     mid = b1_v.shape[1]
     for first in range(0, rows + 2, 5):
         count = min(5, rows + 2 - first)
-        half = (convolve(att3, c1_v, first, count, mid) + b1_v[...]) * 0.5
+        half = (convolve(att3, c1_t, first, count, mid) + b1_v[...]) * 0.5
         cells = (half + half * jnp.tanh(half)).reshape(-1, slab, mid)
         below, above = shifted(cells)
         stacked = jnp.concatenate([below, cells, above], axis=2).astype(BF16)
@@ -227,7 +236,7 @@
     blank(gy == n_gy - 1, hid3, (every_dim, pl.ds(wide + slab, slab), every_dim))
 
     for first in range(0, rows, 4):
-        final = convolve(hid3, c2_v, first, 4, mid) + b2_v[...]
+        final = convolve(hid3, c2_t, first, 4, mid) + b2_v[...]
         result[pl.ds(first * wide, 4 * wide), :mid] = final.reshape(4 * wide, mid)
     pieces = [result[pl.ds(z, rows * cols, stride=slab), :][:, :mid] for z in range(slab)]
     out[...] = jnp.concatenate(pieces, axis=1).astype(BF16)
@@ -259,7 +268,7 @@
     )
     result = pl.pallas_call(
         partial(kernel, (n_lat, n_gx, n_gy, rows, cols, slab)),
-        out_shape=jax.ShapeDtypeStruct((rows * cols, slab * mid), BF16),
+        out_shape=pltpu.VMEM((rows * cols, slab * mid), BF16),
         in_specs=[any_spec] * 8,
         out_specs=pl.BlockSpec(memory_space=pltpu.VMEM),
         scratch_shapes=[
@@ -284,6 +293,8 @@
             pltpu.SemaphoreType.DMA((n_plane,)),
             pltpu.VMEM((n_plane * n_lat * piece, channels), BF16),
             pltpu.VMEM((n_plane * n_lat * piece, 2 * channels), BF16),
+            pltpu.VMEM((9 * channels, 3 * mid), BF16),
+            pltpu.VMEM((9 * mid, 3 * mid), BF16),
         ],
         compiler_params=pltpu.CompilerParams(collective_id=0, has_side_effects=True),
     )(*operands)

time: 18.5 us -> 16.7 us (0.903)
  local copies, waits for them, and re-layouts: 1.57 us -> 0.66 us
  Pallas kernels: 16.7 us -> 15.8 us
    unnamed x1, local copies, waits for them, and re-layouts: 1.57 us -> 0.66 us
    pallas_call x1, Pallas kernels: 16.7 us -> 15.8 us  [shards(): pl.pallas_call(partial(kernel, (n_lat, n_gx, n_gy, rows, cols, slab)), ou...]
where the time goes in v2:
time: 16.7 us; the launch traced here: 16.5 us
  Pallas kernels  15.8 us (95%)
  local copies, waits for them, and re-layouts  0.66 us (4%)
    pallas_call x1, Pallas kernels, shards(): pl.pallas_call(partial(kernel, (n_lat, n_gx, n_gy, rows, cols, slab)), ou...  15.8 us
    unnamed x1, local copies, waits for them, and re-layouts  0.66 us

profile of v2, /device:TPU:0, one launch (start us, length us, event | category | flops | bytes accessed | tf_op | source)
XLA Modules:
  0.0 16.5 jit_solution(4374165265545047458)
XLA Ops:
  0.0 15.8 %shard_map.82 = bf16[128,512]{1,0:T(8,128)(2,1)S(1)} custom-call(bf16[8,1024]{1,0:T(8,128)(2,1)} %latents.1, bf16[1024,128]{1,0:T(8,128)(2,1)} %w_key.1, bf16[1024,128]{1,0:T(8,128)(2,1)} %w_value.1, bf16[8,128,128]{2,1,0:T(8,128)(2,1)} %bitcast.9, bf16[3,192,384]{2,1,0:T(8,128)(2,1)} %bitcast.7, f32[1,64]{1,0:T(1,128)} %bitcast.10, ...), custom_call_target="tpu_custom_call" | custom-call | tf_op jit(solution)/shard_map/pallas_call | solution.py:269
  15.8 0.7 %copy.10 = bf16[8,16,512]{2,1,0:T(8,128)(2,1)} copy(bf16[8,16,512]{2,1,0:T(8,128)(2,1)S(1)} %bitcast.6) | data formatting | bytes 262144

commit v3 on v2

--- a/solution.py
+++ b/solution.py
@@ -61,7 +61,10 @@
     for k in range(1, n_plane):
         pl.semaphore_signal(barrier, inc=1, device_id=plane_device(lax.rem(plane + k, n_plane)), device_id_type=MESH)
     for dx, dy in DIRECTIONS:
-        there = present(row_tile + dx, gy + dy)
+        if dx == 0:
+            continue
+        outer = 0 if dx < 0 else n_gx - 1
+        there = present(row_tile + dx, gy + dy) & (gx == outer)
         awaited = awaited + there.astype(jnp.int32)
 
         @pl.when(there)
@@ -131,6 +134,14 @@
         def _():
             halo_copy(i, dx, dy).wait_recv()
 
+    for k in range(1, n_lat):
+        column_copy(k, lat).wait_send()
+    for k in range(1, n_plane):
+        plane_copy(k, plane).wait_send()
+    for i, (dx, dy) in enumerate(DIRECTIONS):
+        @pl.when(present(row_tile + dx, gy + dy))
+        def _():
+            halo_copy(i, dx, dy).wait_send()
     for k in range(1, n_plane):
         plane_copy(k, lax.rem(plane + n_plane - k, n_plane)).wait_recv()
 
@@ -192,10 +203,8 @@
             attend(s * step, step)
 
     def blank(when, ref, index):
-        @pl.when(when)
-        def _():
-            view = ref.at[index]
-            view[...] = jnp.zeros(view.shape, ref.dtype)
+        cells = ref[index]
+        ref[index] = jnp.where(when, jnp.zeros_like(cells), cells)
 
     every_dim = slice(None)
     blank(row_tile == 0, att3, (pl.ds(0, 2), every_dim, every_dim))
@@ -222,8 +231,8 @@
         )
 
     mid = b1_v.shape[1]
-    for first in range(0, rows + 2, 5):
-        count = min(5, rows + 2 - first)
+    for first in range(0, rows + 2, 2):
+        count = min(2, rows + 2 - first)
         half = (convolve(att3, c1_t, first, count, mid) + b1_v[...]) * 0.5
         cells = (half + half * jnp.tanh(half)).reshape(-1, slab, mid)
         below, above = shifted(cells)
@@ -235,20 +244,11 @@
     blank(gy == 0, hid3, (every_dim, pl.ds(0, slab), every_dim))
     blank(gy == n_gy - 1, hid3, (every_dim, pl.ds(wide + slab, slab), every_dim))
 
-    for first in range(0, rows, 4):
-        final = convolve(hid3, c2_t, first, 4, mid) + b2_v[...]
-        result[pl.ds(first * wide, 4 * wide), :mid] = final.reshape(4 * wide, mid)
+    for first in range(0, rows, 2):
+        final = convolve(hid3, c2_t, first, 2, mid) + b2_v[...]
+        result[pl.ds(first * wide, 2 * wide), :mid] = final.reshape(2 * wide, mid)
     pieces = [result[pl.ds(z, rows * cols, stride=slab), :][:, :mid] for z in range(slab)]
     out[...] = jnp.concatenate(pieces, axis=1).astype(BF16)
-
-    for k in range(1, n_lat):
-        column_copy(k, lat).wait_send()
-    for k in range(1, n_plane):
-        plane_copy(k, plane).wait_send()
-    for i, (dx, dy) in enumerate(DIRECTIONS):
-        @pl.when(present(row_tile + dx, gy + dy))
-        def _():
-            halo_copy(i, dx, dy).wait_send()
 
 
 def shards(sizes, latents, w_key, w_value, queries, conv_one, bias_one, conv_two, bias_two):

time: 16.7 us -> 16.2 us (0.970)
  Pallas kernels: 15.8 us -> 15.3 us
    pallas_call x1, Pallas kernels: 15.8 us -> 15.3 us  [shards(): pl.pallas_call(partial(kernel, (n_lat, n_gx, n_gy, rows, cols, slab)), ou...]
where the time goes in v3:
time: 16.2 us; the launch traced here: 15.9 us
  Pallas kernels  15.3 us (94%)
  local copies, waits for them, and re-layouts  0.66 us (4%)
    pallas_call x1, Pallas kernels, shards(): pl.pallas_call(partial(kernel, (n_lat, n_gx, n_gy, rows, cols, slab)), ou...  15.3 us
    unnamed x1, local copies, waits for them, and re-layouts  0.66 us

profile of v3, /device:TPU:0, one launch (start us, length us, event | category | flops | bytes accessed | tf_op | source)
XLA Modules:
  0.0 15.9 jit_solution(11144700329038825175)
XLA Ops:
  0.0 15.3 %shard_map.82 = bf16[128,512]{1,0:T(8,128)(2,1)S(1)} custom-call(bf16[8,1024]{1,0:T(8,128)(2,1)} %latents.1, bf16[1024,128]{1,0:T(8,128)(2,1)} %w_key.1, bf16[1024,128]{1,0:T(8,128)(2,1)} %w_value.1, bf16[8,128,128]{2,1,0:T(8,128)(2,1)} %bitcast.9, bf16[3,192,384]{2,1,0:T(8,128)(2,1)} %bitcast.7, f32[1,64]{1,0:T(1,128)} %bitcast.10, ...), custom_call_target="tpu_custom_call" | custom-call | tf_op jit(solution)/shard_map/pallas_call | solution.py:269
  15.3 0.7 %copy.10 = bf16[8,16,512]{2,1,0:T(8,128)(2,1)} copy(bf16[8,16,512]{2,1,0:T(8,128)(2,1)S(1)} %bitcast.6) | data formatting | bytes 262144
